TPU v7x, 32 devices: a whole 2x2x4 slice. The times are simulated.
32 devices in a mesh: tx: 2 (over y), ty: 4 (over z), sl: 4 (over x, core).
Axes of the slice: x: 2, y: 2, z: 4, core: 2. Of those that a mesh axis runs over, the one named last changes fastest.
Arguments:
- object_field: float32 [8, 2, 512, 1024], P('sl', None, 'tx', 'ty'), may hold values from -0.4 to 1.2, as said below
- illumination: float32 [2, 256, 256], replicated, may hold values from -5 to 5
- positions: int32 [2, 4, 1, 2], P('tx', 'ty'), may hold values from 0 to 255
- measured: float32 [2, 4, 1, 256, 256], P('tx', 'ty'), may hold values from 0.05 to 1.5
Outputs:
- updated: float32 [8, 2, 512, 1024], P('sl', None, 'tx', 'ty')
Inputs may be any that keep to these rules, and one draw needn't show every extreme that they name: `object_field`: real parts lie between 0.6 and 1.2, imaginary parts between -0.4 and 0.4.
All inputs are finite; a program needn't handle non-finite values.
Results may differ from a plain program's by a relative error of at most 0.0003.
Values sent between devices are 32-bit elements; how exact they have to be, the bound alone decides.
A program may use at most 128 MiB of HBM per device.

v0:
```python
import math

import jax
import jax.numpy as jnp
from jax import lax
from jax.sharding import PartitionSpec as P

PRECISE = lax.Precision.HIGHEST
STEP_SIZE = 0.5


def padded(cells, sides, width):
    for axis, dim in sides:
        count = lax.axis_size(axis)
        head = lax.slice_in_dim(cells, 0, width, axis=dim)
        tail = lax.slice_in_dim(cells, cells.shape[dim] - width, cells.shape[dim], axis=dim)
        cells = jnp.concatenate(
            [
                lax.ppermute(tail, axis, [(i, (i + 1) % count) for i in range(count)]),
                cells,
                lax.ppermute(head, axis, [((i + 1) % count, i) for i in range(count)]),
            ],
            axis=dim,
        )
    return cells


def shifted_2(x, axis, by):
    size = lax.axis_size(axis)
    pairs = [(i, i + by) for i in range(size) if 0 <= i + by < size]
    return lax.ppermute(x, axis, pairs)


def from_left(matrix, wave_field):

    def product(left_matrix, right_matrix):
        return jnp.einsum("jk,bkl->bjl", left_matrix, right_matrix, precision=PRECISE)

    real_m, imag_m = (matrix[0], matrix[1])
    real_w, imag_w = (wave_field[:, 0], wave_field[:, 1])
    return jnp.stack(
        [
            product(real_m, real_w) - product(imag_m, imag_w),
            product(real_m, imag_w) + product(imag_m, real_w),
        ],
        axis=1,
    )


def from_right(wave_field, matrix):

    def product(left_matrix, right_matrix):
        return jnp.einsum("bjk,kl->bjl", left_matrix, right_matrix, precision=PRECISE)

    real_m, imag_m = (matrix[0], matrix[1])
    real_w, imag_w = (wave_field[:, 0], wave_field[:, 1])
    return jnp.stack(
        [
            product(real_w, real_m) - product(imag_w, imag_m),
            product(real_w, imag_m) + product(imag_w, real_m),
        ],
        axis=1,
    )


def sandwich(matrix, wave_field):
    return from_right(from_left(matrix, wave_field), matrix)


def times_plain(first_term, second_term):
    real_a, imag_a = (first_term[..., 0, :, :], first_term[..., 1, :, :])
    real_b, imag_b = (second_term[..., 0, :, :], second_term[..., 1, :, :])
    return jnp.stack(
        [real_a * real_b - imag_a * imag_b, real_a * imag_b + imag_a * real_b], axis=-3
    )


def times_conj(first_term, second_term):
    real_a, imag_a = (first_term[..., 0, :, :], first_term[..., 1, :, :])
    real_b, imag_b = (second_term[..., 0, :, :], second_term[..., 1, :, :])
    return jnp.stack(
        [real_a * real_b + imag_a * imag_b, real_a * imag_b - imag_a * real_b], axis=-3
    )


def build_tables(length):
    indices = jnp.arange(length, dtype=jnp.int32)
    products = indices[:, None] * indices[None, :] % length
    angles = products.astype(jnp.float32) * (-2.0 * math.pi / length)
    factor = 1.0 / math.sqrt(length)
    forward = jnp.stack([jnp.cos(angles), jnp.sin(angles)]) * factor
    backward = jnp.stack([jnp.cos(angles), -jnp.sin(angles)]) * factor
    shifted = jnp.where(indices < length // 2, indices, indices - length)
    phases = (shifted * shifted % (4 * length)).astype(jnp.float32) * (-math.pi / (2 * length))
    cos_row = jnp.cos(phases)[None, :]
    sin_row = jnp.sin(phases)[None, :]
    columns = jnp.stack(
        [
            backward[0] * cos_row - backward[1] * sin_row,
            backward[0] * sin_row + backward[1] * cos_row,
        ]
    )
    spread = from_left(columns, forward[None])[0]
    spread_conj = jnp.stack([spread[0], -spread[1]])
    return (forward, backward, spread, spread_conj)


def detector_gradient(wave_field, measured_part, forward, backward):
    farfield = sandwich(forward, wave_field)
    intensity = farfield[:, 0] * farfield[:, 0] + farfield[:, 1] * farfield[:, 1]
    residual = (intensity - measured_part)[:, None]
    return sandwich(backward, residual * farfield)


def take_windows(field_part, starts, probe_width):

    def one_window(start_pair):
        return lax.dynamic_slice(
            field_part, (jnp.int32(0), start_pair[0], start_pair[1]), (2, probe_width, probe_width)
        )

    return jax.vmap(one_window)(starts)


def section_forward(extended, wave_field, starts, spread, probe_width):
    saved_waves = []
    for layer_index in range(extended.shape[0]):
        saved_waves.append(wave_field)
        windows = take_windows(extended[layer_index], starts, probe_width)
        wave_field = sandwich(spread, times_plain(windows, wave_field))
    return (wave_field, jnp.stack(saved_waves, axis=1))


def section_backward(
    extended, adjoint_wave, saved_waves, starts, gradient_sum, spread_conj, probe_width
):
    anchor = jnp.int32(0)
    for layer_index in reversed(range(extended.shape[0])):
        inner_grad = sandwich(spread_conj, adjoint_wave)
        windows = take_windows(extended[layer_index], starts, probe_width)
        contrib = times_conj(saved_waves[:, layer_index], inner_grad)
        corner_at = (jnp.int32(layer_index), anchor, starts[0, 0], starts[0, 1])
        current = lax.dynamic_slice(gradient_sum, corner_at, (1, 2, probe_width, probe_width))
        gradient_sum = lax.dynamic_update_slice(gradient_sum, current + contrib[0][None], corner_at)
        adjoint_wave = times_conj(windows, inner_grad)
    return (adjoint_wave, gradient_sum)


def fold_rims(padded_grad, axis_dim, half_width):
    full_length = padded_grad.shape[axis_dim]
    tile_length = full_length - 4 * half_width
    middle = lax.slice_in_dim(
        padded_grad, 2 * half_width, 2 * half_width + tile_length, axis=axis_dim
    )
    upper_rim = lax.slice_in_dim(padded_grad, 0, half_width, axis=axis_dim)
    lower_rim = lax.slice_in_dim(padded_grad, full_length - half_width, full_length, axis=axis_dim)
    upper_pad = [(0, 0)] * padded_grad.ndim
    lower_pad = [(0, 0)] * padded_grad.ndim
    upper_pad[axis_dim] = (0, tile_length - half_width)
    lower_pad[axis_dim] = (tile_length - half_width, 0)
    return middle + jnp.pad(upper_rim, upper_pad) + jnp.pad(lower_rim, lower_pad)


def body(object_field, illumination, positions, measured):
    sl_count = lax.axis_size("sl")
    my_section = lax.axis_index("sl")
    last_section = sl_count - 1
    probe_width = illumination.shape[-1]
    half_width = probe_width // 2
    extended = padded(object_field, (("tx", 2), ("ty", 3)), half_width)
    offsets = positions.reshape(-1, 2)
    intensities = measured.reshape(-1, probe_width, probe_width)
    probe_count = offsets.shape[0]
    layers = extended.shape[0]
    forward, backward, spread, spread_conj = build_tables(probe_width)
    groups = probe_count // probe_count
    moments = sl_count + groups - 1
    wave_shape = (probe_count, 2, probe_width, probe_width)
    launch = jnp.broadcast_to(illumination, wave_shape)
    incoming = jnp.zeros(wave_shape, jnp.float32)
    saved_all = jnp.zeros((probe_count, layers, 2, probe_width, probe_width), jnp.float32)
    exit_grads = jnp.zeros((probe_count, 2, probe_width, probe_width), jnp.float32)
    for moment in range(moments):
        micro_index = moment - my_section
        active = (micro_index >= 0) & (micro_index < groups)
        first_row = jnp.clip(micro_index, 0, groups - 1) * probe_count
        starts = offsets
        source = jnp.where(my_section == 0, launch, incoming)

        def run_forward(operands):
            wave_in, saved_now, exits_now = operands
            wave_out, saved_waves = section_forward(extended, wave_in, starts, spread, probe_width)
            saved_now = lax.dynamic_update_slice(saved_now, saved_waves, (first_row, 0, 0, 0, 0))

            def record_exit(exits_old):
                return detector_gradient(wave_out, intensities, forward, backward)

            def keep_exit(exits_old):
                return exits_old

            exits_now = lax.cond(my_section == last_section, record_exit, keep_exit, exits_now)
            return (wave_out, saved_now, exits_now)

        def skip_forward(operands):
            return (jnp.zeros_like(operands[0]), operands[1], operands[2])

        outgoing, saved_all, exit_grads = lax.cond(
            active, run_forward, skip_forward, (source, saved_all, exit_grads)
        )
        if moment < moments - 1:
            incoming = shifted_2(outgoing, "sl", 1)
    incoming = jnp.zeros(wave_shape, jnp.float32)
    gradient_sum = jnp.zeros(extended.shape, jnp.float32)
    for moment in range(moments):
        micro_index = moment - (last_section - my_section)
        active = (micro_index >= 0) & (micro_index < groups)
        first_row = jnp.clip(micro_index, 0, groups - 1) * probe_count
        starts = offsets
        source = jnp.where(my_section == last_section, exit_grads, incoming)

        def run_backward(operands):
            adjoint_in, sum_now = operands
            return section_backward(
                extended, adjoint_in, saved_all, starts, sum_now, spread_conj, probe_width
            )

        def skip_backward(operands):
            return (jnp.zeros_like(operands[0]), operands[1])

        outgoing, gradient_sum = lax.cond(
            active, run_backward, skip_backward, (source, gradient_sum)
        )
        if moment < moments - 1:
            incoming = shifted_2(outgoing, "sl", -1)
    rows_done = fold_rims(padded(gradient_sum, (("tx", 2),), half_width), 2, half_width)
    tile_gradient = fold_rims(padded(rows_done, (("ty", 3),), half_width), 3, half_width)
    return object_field - STEP_SIZE * tile_gradient


def solution(mesh):
    placed = (
        P("sl", None, "tx", "ty"),
        P(),
        P("tx", "ty", None, None),
        P("tx", "ty", None, None, None),
    )
    return jax.shard_map(
        body, mesh=mesh, in_specs=placed, out_specs=P("sl", None, "tx", "ty"), check_vma=False
    )
```

profile of v0, /device:TPU:0, one launch (start us, length us, event | category | flops | bytes accessed | tf_op | source)
XLA Modules:
  0.0 469.0 jit_solution(17628848253426892498)
XLA Ops:
  0.0 2.3 fusion.378
  2.3 3.0 collective-permute-start
  8.5 9.8 %collective-permute-done = f32[2,2,128,256]{3,2,1,0:T(8,128)} collective-permute-done((f32[2,2,128,256]{3,2,1,0:T(8,128)}, f32[2,2,128,256]{3,2,1,0:T(8,128)}, u32[]{:S(2)}, u32[]{:S(2)}) %collective-permute-start) | collective-permute-done | bytes 524320 | tf_op jit(solution)/shard_map/ppermute | solution.py:19
  19.5 9.2 %collective-permute-done.1 = f32[2,2,128,256]{3,2,1,0:T(8,128)} collective-permute-done((f32[2,2,128,256]{3,2,1,0:T(8,128)}, f32[2,2,128,256]{3,2,1,0:T(8,128)}, u32[]{:S(2)}, u32[]{:S(2)}) %collective-permute-start.1) | collective-permute-done | bytes 524320 | tf_op jit(solution)/shard_map/ppermute | solution.py:21
  29.9 3.9 collective-permute-start.3
  36.3 21.1 %collective-permute-done.3 = f32[2,2,512,128]{3,2,1,0:T(8,128)S(1)} collective-permute-done((f32[2,2,512,128]{3,2,1,0:T(8,128)S(1)}, f32[2,2,512,128]{3,2,1,0:T(8,128)S(1)}, u32[]{:S(2)}, u32[]{:S(2)}) %collective-permute-start.3) | collective-permute-done | bytes 1048608 | tf_op jit(solution)/shard_map/ppermute | solution.py:21
  57.4 21.3 %collective-permute-done.2 = f32[2,2,512,128]{3,2,1,0:T(8,128)S(1)} collective-permute-done((f32[2,2,512,128]{3,2,1,0:T(8,128)S(1)}, f32[2,2,512,128]{3,2,1,0:T(8,128)S(1)}, u32[]{:S(2)}, u32[]{:S(2)}) %collective-permute-start.2) | collective-permute-done | bytes 1048608 | tf_op jit(solution)/shard_map/ppermute | solution.py:19
  79.2 2.0 copy-done
  81.2 30.7 %conditional.12 = (f32[1,2,256,256]{3,2,1,0:T(8,128)}, f32[1,2,2,256,256]{4,3,2,1,0:T(8,128)S(1)}, f32[1,2,256,256]{3,2,1,0:T(8,128)}) conditional(s32[]{:T(128)} %convert_element_type.111, () %tuple.102, (f32[2,2,512,512]{3,2,1,0:T(8,128)S(1)}, s32[1,2]{1,0:T(1,128)S(1)}, pred[]{:T(512)}, f32[2,256,256]{2,1,0:T(8,128)S(1)}, ...), branch_computations={%region_0.1_spmd, %region_1.4_spmd} | conditional | flops 6445596672 | bytes 54001924 | solution.py:207
  82.5 2.5 fusion.360
  111.9 2.1 collective-permute-start.4
  115.0 11.8 %conditional.13 = (f32[1,2,256,256]{3,2,1,0:T(8,128)}, f32[1,2,2,256,256]{4,3,2,1,0:T(8,128)S(1)}, f32[1,2,256,256]{3,2,1,0:T(8,128)}) conditional(s32[]{:T(128)} %convert_element_type.110, (f32[1,2,2,256,256]{4,3,2,1,0:T(8,128)S(1)}, f32[1,2,256,256]{3,2,1,0:T(8,128)}) %tuple.104, (f32[2,2,512,512]{3,2,1,0:T(8,128)}, s32[1,2]{1,0:T(1,128)S(1)}, ...), branch_computations={%region_4.5_spmd, %region_5.8_spmd} | conditional | flops 6445596672 | bytes 57147708 | solution.py:207
  126.9 25.2 %collective-permute-start.5 = (f32[1,2,256,256]{3,2,1,0:T(8,128)}, f32[1,2,256,256]{3,2,1,0:T(8,128)}, u32[]{:S(2)}, u32[]{:S(2)}) collective-permute-start(f32[1,2,256,256]{3,2,1,0:T(8,128)} %get-tuple-element.470), channel_id=1, source_target_pairs={{0,1},{1,2},{2,3},{4,5},{5,6},{6,7},{8,9},{9,10},{10,11},{12,13},{... | collective-permute-start | bytes 1572872 | tf_op jit(solution)/shard_map/ppermute | solution.py:31
  153.1 8.9 %conditional.14 = (f32[1,2,256,256]{3,2,1,0:T(8,128)}, f32[1,2,2,256,256]{4,3,2,1,0:T(8,128)S(1)}, f32[1,2,256,256]{3,2,1,0:T(8,128)}) conditional(s32[]{:T(128)} %convert_element_type.109, (f32[1,2,2,256,256]{4,3,2,1,0:T(8,128)S(1)}, f32[1,2,256,256]{3,2,1,0:T(8,128)}) %tuple.106, (f32[2,2,512,512]{3,2,1,0:T(8,128)}, s32[1,2]{1,0:T(1,128)S(1)}, ...), branch_computations={%region_8.9_spmd, %region_9.12_spmd} | conditional | flops 6445596672 | bytes 57147708 | solution.py:207
  162.0 7.3 %collective-permute-start.6 = (f32[1,2,256,256]{3,2,1,0:T(8,128)}, f32[1,2,256,256]{3,2,1,0:T(8,128)}, u32[]{:S(2)}, u32[]{:S(2)}) collective-permute-start(f32[1,2,256,256]{3,2,1,0:T(8,128)} %get-tuple-element.473), channel_id=1, source_target_pairs={{0,1},{1,2},{2,3},{4,5},{5,6},{6,7},{8,9},{9,10},{10,11},{12,13},{... | collective-permute-start | bytes 1572872 | tf_op jit(solution)/shard_map/ppermute | solution.py:31
  170.3 8.8 %conditional.15 = ((f32[1,2,2,256,256]{4,3,2,1,0:T(8,128)S(1)}, f32[1,2,256,256]{3,2,1,0:T(8,128)})) conditional(s32[]{:T(128)} %convert_element_type.108, (f32[1,2,2,256,256]{4,3,2,1,0:T(8,128)S(1)}, f32[1,2,256,256]{3,2,1,0:T(8,128)}) %tuple.108, (pred[]{:T(512)}, f32[1,2,256,256]{3,2,1,0:T(8,128)}, f32[1,2,256,256]{3,2,1,0:T(8,128)}, ...), branch_computations={%region_12.13_spmd, %region_13.16_spmd} | conditional | flops 6445596672 | bytes 63963636 | solution.py:207
  179.1 3.4 conditional.16
  180.0 2.5 broadcast_in_dim.65
  183.8 34.2 %collective-permute-done.7 = f32[1,2,256,256]{3,2,1,0:T(8,128)S(1)} collective-permute-done((f32[1,2,256,256]{3,2,1,0:T(8,128)}, f32[1,2,256,256]{3,2,1,0:T(8,128)S(1)}, u32[]{:S(2)}, u32[]{:S(2)}) %collective-permute-start.7) | collective-permute-done | bytes 524320 | tf_op jit(solution)/shard_map/ppermute | solution.py:31
  220.6 10.1 %collective-permute-done.8 = f32[1,2,256,256]{3,2,1,0:T(8,128)S(1)} collective-permute-done((f32[1,2,256,256]{3,2,1,0:T(8,128)}, f32[1,2,256,256]{3,2,1,0:T(8,128)S(1)}, u32[]{:S(2)}, u32[]{:S(2)}) %collective-permute-start.8) | collective-permute-done | bytes 524320 | tf_op jit(solution)/shard_map/ppermute | solution.py:31
  233.1 152.5 %collective-permute-done.9 = f32[1,2,256,256]{3,2,1,0:T(8,128)S(1)} collective-permute-done((f32[1,2,256,256]{3,2,1,0:T(8,128)}, f32[1,2,256,256]{3,2,1,0:T(8,128)S(1)}, u32[]{:S(2)}, u32[]{:S(2)}) %collective-permute-start.9) | collective-permute-done | bytes 524320 | tf_op jit(solution)/shard_map/ppermute | solution.py:31
  385.5 36.8 %conditional.19 = (f32[2,2,512,512]{3,2,1,0:T(8,128)}) conditional(s32[]{:T(128)} %convert_element_type.104, f32[2,2,512,512]{3,2,1,0:T(8,128)} %get-tuple-element.480, (s32[1,2]{1,0:T(1,128)S(1)}, f32[2,2,512,512]{3,2,1,0:T(8,128)}, f32[1,2,2,256,256]{4,3,2,1,0:T(8,128)S(1)}, pred[]{:T(512)}, f32[1,2,256,256]{3,2,1,0:T(8,128)}, ...), branch_computations={%region_22.23_spmd, %region_23.24_spmd} | conditional | flops 3223584768 | bytes 47710436 | solution.py:230
  395.8 1.8 multiply_subtract_fusion.11
  402.7 6.7 %dynamic_update_slice.26 = f32[2,2,512,512]{3,2,1,0:T(8,128)} dynamic-update-slice(f32[2,2,512,512]{3,2,1,0:T(8,128)} %get-tuple-element.439, f32[1,2,256,256]{3,2,1,0:T(8,128)S(1)} %maximum_add_fusion.5, s32[]{:T(128)} %constant.138.clone, s32[]{:T(128)} %constant.160.clone, s32[]{:T(128)S(6)} %select_n.248, s32[]{:T(128)S(6)} %select_n.249) | dynamic-update-slice | bytes 1048580 | tf_op jit(solution)/shard_map/cond/branch_1_fun/dynamic_update_slice | solution.py:144
  415.6 6.7 %dynamic_update_slice.27 = f32[2,2,512,512]{3,2,1,0:T(8,128)} dynamic-update-slice(f32[2,2,512,512]{3,2,1,0:T(8,128)} %dynamic_update_slice.26, f32[1,2,256,256]{3,2,1,0:T(8,128)S(1)} %maximum_add_fusion.6, s32[]{:T(128)} %constant.160.clone, s32[]{:T(128)} %constant.160.clone, s32[]{:T(128)S(6)} %select_n.248, s32[]{:T(128)S(6)} %select_n.249) | dynamic-update-slice | bytes 1048580 | tf_op jit(solution)/shard_map/cond/branch_1_fun/dynamic_update_slice | solution.py:144
  424.1 2.0 collective-permute-start.10
  426.2 12.8 %collective-permute-done.11 = f32[2,2,128,512]{3,2,1,0:T(8,128)S(1)} collective-permute-done((f32[2,2,128,512]{3,2,1,0:T(8,128)S(1)}, f32[2,2,128,512]{3,2,1,0:T(8,128)S(1)}, u32[]{:S(2)}, u32[]{:S(2)}) %collective-permute-start.11) | collective-permute-done | bytes 1048608 | tf_op jit(solution)/shard_map/ppermute | solution.py:21
  438.9 11.2 %collective-permute-done.10 = f32[2,2,128,512]{3,2,1,0:T(8,128)S(1)} collective-permute-done((f32[2,2,128,512]{3,2,1,0:T(8,128)S(1)}, f32[2,2,128,512]{3,2,1,0:T(8,128)S(1)}, u32[]{:S(2)}, u32[]{:S(2)}) %collective-permute-start.10) | collective-permute-done | bytes 1048608 | tf_op jit(solution)/shard_map/ppermute | solution.py:19
  450.2 2.1 fusion.330
  452.4 2.0 collective-permute-start.12
  454.4 7.2 %collective-permute-done.13 = f32[2,2,256,128]{3,2,1,0:T(8,128)S(1)} collective-permute-done((f32[2,2,256,128]{3,2,1,0:T(8,128)S(1)}, f32[2,2,256,128]{3,2,1,0:T(8,128)S(1)}, u32[]{:S(2)}, u32[]{:S(2)}) %collective-permute-start.13) | collective-permute-done | bytes 524320 | tf_op jit(solution)/shard_map/ppermute | solution.py:21
  461.6 5.9 %collective-permute-done.12 = f32[2,2,256,128]{3,2,1,0:T(8,128)S(1)} collective-permute-done((f32[2,2,256,128]{3,2,1,0:T(8,128)S(1)}, f32[2,2,256,128]{3,2,1,0:T(8,128)S(1)}, u32[]{:S(2)}, u32[]{:S(2)}) %collective-permute-start.12) | collective-permute-done | bytes 524320 | tf_op jit(solution)/shard_map/ppermute | solution.py:19
  (98 shorter events, 55.5 us)
Async XLA Ops:
  2.3 16.0 %collective-permute-start = (f32[2,2,128,256]{3,2,1,0:T(8,128)}, f32[2,2,128,256]{3,2,1,0:T(8,128)}, u32[]{:S(2)}, u32[]{:S(2)}) collective-permute-start(f32[2,2,128,256]{3,2,1,0:T(8,128)} %get-tuple-element.840), channel_id=1, source_target_pairs={{0,16},{16,0},{1,17},{17,1},{2,18},{18,2},{3,19},{19,3},{4,20},{20... | collective-permute-start | bytes 1572872 | tf_op jit(solution)/shard_map/ppermute | solution.py:19
  5.2 23.5 %collective-permute-start.1 = (f32[2,2,128,256]{3,2,1,0:T(8,128)}, f32[2,2,128,256]{3,2,1,0:T(8,128)}, u32[]{:S(2)}, u32[]{:S(2)}) collective-permute-start(f32[2,2,128,256]{3,2,1,0:T(8,128)} %get-tuple-element.839), channel_id=1, source_target_pairs={{16,0},{0,16},{17,1},{1,17},{18,2},{2,18},{19,3},{3,19},{20,4},{4,... | collective-permute-start | bytes 1572872 | tf_op jit(solution)/shard_map/ppermute | solution.py:21
  7.3 12.0 %copy-start.6 = (f32[2,2,256,256]{3,2,1,0:T(8,128)S(1)}, f32[2,2,256,256]{3,2,1,0:T(8,128)}, u32[]{:S(2)}) copy-start(f32[2,2,256,256]{3,2,1,0:T(8,128)} %param.28) | copy-start | bytes 3145732
  29.9 27.5 %collective-permute-start.3 = (f32[2,2,512,128]{3,2,1,0:T(8,128)S(1)}, f32[2,2,512,128]{3,2,1,0:T(8,128)S(1)}, u32[]{:S(2)}, u32[]{:S(2)}) collective-permute-start(f32[2,2,512,128]{3,2,1,0:T(8,128)S(1)} %get-tuple-element.838), channel_id=1, source_target_pairs={{4,0},{8,4},{12,8},{0,12},{5,1},{9,5},{13,9},{1,13},{6,2},{10,6},{... | collective-permute-start | bytes 3145736 | tf_op jit(solution)/shard_map/ppermute | solution.py:21
  33.8 44.9 %collective-permute-start.2 = (f32[2,2,512,128]{3,2,1,0:T(8,128)S(1)}, f32[2,2,512,128]{3,2,1,0:T(8,128)S(1)}, u32[]{:S(2)}, u32[]{:S(2)}) collective-permute-start(f32[2,2,512,128]{3,2,1,0:T(8,128)S(1)} %get-tuple-element.837), channel_id=1, source_target_pairs={{0,4},{4,8},{8,12},{12,0},{1,5},{5,9},{9,13},{13,1},{2,6},{6,10},{... | collective-permute-start | bytes 3145736 | tf_op jit(solution)/shard_map/ppermute | solution.py:19
  35.6 43.6 %copy-start.27 = (f32[256,256]{1,0:T(8,128)}, f32[256,256]{1,0:T(8,128)S(1)}, u32[]{:S(2)}) copy-start(f32[256,256]{1,0:T(8,128)S(1)} %convolution_add_fusion.47) | copy-start | bytes 786436
  36.3 42.9 %copy-start.8 = (f32[2,256,256]{2,1,0:T(8,128)S(1)}, f32[2,256,256]{2,1,0:T(8,128)}, u32[]{:S(2)}) copy-start(f32[2,256,256]{2,1,0:T(8,128)} %param.29) | copy-start | bytes 1572868
  36.3 42.9 %copy-start.32 = (s32[1,1,1,2]{3,2,1,0:T(1,128)S(1)}, s32[1,1,1,2]{3,2,1,0:T(1,128)}, u32[]{:S(2)}) copy-start(s32[1,1,1,2]{3,2,1,0:T(1,128)} %param.30) | copy-start | bytes 28
  79.2 2.0 copy-start
  100.8 2.1 copy-start.28
  111.9 3.2 collective-permute-start.4
  126.9 26.2 %collective-permute-start.5 = (f32[1,2,256,256]{3,2,1,0:T(8,128)}, f32[1,2,256,256]{3,2,1,0:T(8,128)}, u32[]{:S(2)}, u32[]{:S(2)}) collective-permute-start(f32[1,2,256,256]{3,2,1,0:T(8,128)} %get-tuple-element.470), channel_id=1, source_target_pairs={{0,1},{1,2},{2,3},{4,5},{5,6},{6,7},{8,9},{9,10},{10,11},{12,13},{... | collective-permute-start | bytes 1572872 | tf_op jit(solution)/shard_map/ppermute | solution.py:31
  162.0 8.3 %collective-permute-start.6 = (f32[1,2,256,256]{3,2,1,0:T(8,128)}, f32[1,2,256,256]{3,2,1,0:T(8,128)}, u32[]{:S(2)}, u32[]{:S(2)}) collective-permute-start(f32[1,2,256,256]{3,2,1,0:T(8,128)} %get-tuple-element.473), channel_id=1, source_target_pairs={{0,1},{1,2},{2,3},{4,5},{5,6},{6,7},{8,9},{9,10},{10,11},{12,13},{... | collective-permute-start | bytes 1572872 | tf_op jit(solution)/shard_map/ppermute | solution.py:31
  182.5 35.5 %collective-permute-start.7 = (f32[1,2,256,256]{3,2,1,0:T(8,128)}, f32[1,2,256,256]{3,2,1,0:T(8,128)S(1)}, u32[]{:S(2)}, u32[]{:S(2)}) collective-permute-start(f32[1,2,256,256]{3,2,1,0:T(8,128)} %get-tuple-element.477), channel_id=1, source_target_pairs={{1,0},{2,1},{3,2},{5,4},{6,5},{7,6},{9,8},{10,9},{11,10},{13,12},{... | collective-permute-start | bytes 1572872 | tf_op jit(solution)/shard_map/ppermute | solution.py:31
  219.3 11.4 %collective-permute-start.8 = (f32[1,2,256,256]{3,2,1,0:T(8,128)}, f32[1,2,256,256]{3,2,1,0:T(8,128)S(1)}, u32[]{:S(2)}, u32[]{:S(2)}) collective-permute-start(f32[1,2,256,256]{3,2,1,0:T(8,128)} %get-tuple-element.479), channel_id=1, source_target_pairs={{1,0},{2,1},{3,2},{5,4},{6,5},{7,6},{9,8},{10,9},{11,10},{13,12},{... | collective-permute-start | bytes 1572872 | tf_op jit(solution)/shard_map/ppermute | solution.py:31
  231.8 153.8 %collective-permute-start.9 = (f32[1,2,256,256]{3,2,1,0:T(8,128)}, f32[1,2,256,256]{3,2,1,0:T(8,128)S(1)}, u32[]{:S(2)}, u32[]{:S(2)}) collective-permute-start(f32[1,2,256,256]{3,2,1,0:T(8,128)} %get-tuple-element.481), channel_id=1, source_target_pairs={{1,0},{2,1},{3,2},{5,4},{6,5},{7,6},{9,8},{10,9},{11,10},{13,12},{... | collective-permute-start | bytes 1572872 | tf_op jit(solution)/shard_map/ppermute | solution.py:31
  386.4 3.0 copy-start.4
  424.1 14.9 %collective-permute-start.11 = (f32[2,2,128,512]{3,2,1,0:T(8,128)S(1)}, f32[2,2,128,512]{3,2,1,0:T(8,128)S(1)}, u32[]{:S(2)}, u32[]{:S(2)}) collective-permute-start(f32[2,2,128,512]{3,2,1,0:T(8,128)S(1)} %get-tuple-element.834), channel_id=1, source_target_pairs={{16,0},{0,16},{17,1},{1,17},{18,2},{2,18},{19,3},{3,19},{20,4},{4,... | collective-permute-start | bytes 3145736 | tf_op jit(solution)/shard_map/ppermute | solution.py:21
  424.1 26.0 %collective-permute-start.10 = (f32[2,2,128,512]{3,2,1,0:T(8,128)S(1)}, f32[2,2,128,512]{3,2,1,0:T(8,128)S(1)}, u32[]{:S(2)}, u32[]{:S(2)}) collective-permute-start(f32[2,2,128,512]{3,2,1,0:T(8,128)S(1)} %get-tuple-element.833), channel_id=1, source_target_pairs={{0,16},{16,0},{1,17},{17,1},{2,18},{18,2},{3,19},{19,3},{4,20},{20... | collective-permute-start | bytes 3145736 | tf_op jit(solution)/shard_map/ppermute | solution.py:19
  452.2 15.3 %copy-start.7 = (f32[2,2,256,256]{3,2,1,0:T(8,128)S(1)}, f32[2,2,256,256]{3,2,1,0:T(8,128)}, u32[]{:S(2)}) copy-start(f32[2,2,256,256]{3,2,1,0:T(8,128)} %param.28) | copy-start | bytes 3145732
  452.3 9.2 %collective-permute-start.13 = (f32[2,2,256,128]{3,2,1,0:T(8,128)S(1)}, f32[2,2,256,128]{3,2,1,0:T(8,128)S(1)}, u32[]{:S(2)}, u32[]{:S(2)}) collective-permute-start(f32[2,2,256,128]{3,2,1,0:T(8,128)S(1)} %get-tuple-element.836), channel_id=1, source_target_pairs={{4,0},{8,4},{12,8},{0,12},{5,1},{9,5},{13,9},{1,13},{6,2},{10,6},{... | collective-permute-start | bytes 1572872 | tf_op jit(solution)/shard_map/ppermute | solution.py:21
  452.4 15.1 %collective-permute-start.12 = (f32[2,2,256,128]{3,2,1,0:T(8,128)S(1)}, f32[2,2,256,128]{3,2,1,0:T(8,128)S(1)}, u32[]{:S(2)}, u32[]{:S(2)}) collective-permute-start(f32[2,2,256,128]{3,2,1,0:T(8,128)S(1)} %get-tuple-element.835), channel_id=1, source_target_pairs={{0,4},{4,8},{8,12},{12,0},{1,5},{5,9},{9,13},{13,1},{2,6},{6,10},{... | collective-permute-start | bytes 1572872 | tf_op jit(solution)/shard_map/ppermute | solution.py:19
where the time goes:
time: 475 us; the launch traced here: 469 us
  waiting for transfers between devices  298 us (63%)
  starting transfers between devices  49.5 us (10%)
  loops' own time  48.8 us (10%)
  local copies, waits for them, and re-layouts  34.8 us (7%)
  matrix products  23.8 us (5%)
  other arithmetic  14 us (3%)
    ppermute x6, waiting for transfers between devices, shifted_2(): return lax.ppermute(x, axis, pairs)  199 us
    ppermute x4, waiting for transfers between devices, padded(): lax.ppermute(head, axis, [((i + 1) % count, i) for i in range(count)])  50.3 us
    ppermute x4, waiting for transfers between devices, padded(): lax.ppermute(tail, axis, [(i, (i + 1) % count) for i in range(count)])  48.2 us
    another operation x4, loops' own time, body(): lax.cond(active, run_forward, skip_forward, (source, saved_all, exit_grads))  40.4 us
    ppermute x6, starting transfers between devices, shifted_2(): return lax.ppermute(x, axis, pairs)  38.5 us
    dynamic_update_slice x2, local copies, waits for them, and re-layouts, section_backward(): lax.dynamic_update_slice(gradient_sum, current + contrib[0][None], corner...  13.5 us
    dot_general x16, matrix products, product(): jnp.einsum('bjk,kl->bjl', left_matrix, right_matrix, precision=PRECISE)  12 us
    dot_general x20, matrix products, product(): jnp.einsum('jk,bkl->bjl', left_matrix, right_matrix, precision=PRECISE)  11.9 us
  transfers between devices with their start and end apart: 14, of which 14 were waited for; matrix products, arithmetic and copies ran while one was open for 2% of the time, Pallas kernels for 0%

commit v1 on v0

v1 whole, which is shorter than its diff:
```python
import functools

import jax
import jax.numpy as jnp
import ml_dtypes
import numpy as np
from jax import lax
from jax.experimental import pallas as pl
from jax.experimental.pallas import tpu as pltpu
from jax.sharding import PartitionSpec as P

STEP_SIZE = 0.5
MESH = pl.DeviceIdType.MESH


def high_low(x):
    high = x.astype(np.float32).astype(ml_dtypes.bfloat16)
    low = (x - high.astype(np.float64)).astype(np.float32).astype(ml_dtypes.bfloat16)
    return high, low


def build_tables(length):
    k = np.arange(length)
    angles = (np.outer(k, k) % length) * (-2.0 * np.pi / length)
    forward = np.exp(1j * angles) / np.sqrt(length)
    q = np.where(k < length // 2, k, k - length)
    phases = np.exp(-1j * np.pi * (q * q % (4 * length)) / (2 * length))
    spread = (np.conj(forward) * phases[None, :]) @ forward
    both = []
    for matrix in (spread, forward):
        real_h, real_l = high_low(matrix.real)
        imag_h, imag_l = high_low(matrix.imag)
        both.append(np.stack([real_h, imag_h, real_l, imag_l]))
    return np.stack(both)


def split(x):
    high = x.astype(jnp.bfloat16)
    low = (x - high.astype(jnp.float32)).astype(jnp.bfloat16)
    return high, low


def dot(a, b):
    return jnp.dot(a, b, preferred_element_type=jnp.float32)


def kernel(
    counts,
    obj,
    ill,
    pos,
    meas,
    tab,
    out,
    t_left,
    t_right,
    ybuf,
    zs,
    zr,
    win,
    psi,
    adj,
    term,
    gzs,
    gzr,
    gys,
    gyr,
    posbuf,
    y_s,
    y_r,
    z_s,
    z_r,
    gz_s,
    gz_r,
    gy_s,
    gy_r,
    p_s,
    p_r,
    w_s,
    w_r,
):
    nx, ny, ns = counts
    layers = obj.shape[0]
    width = obj.shape[-1]
    half = width // 2
    x = lax.axis_index("tx")
    y = lax.axis_index("ty")
    s_me = lax.axis_index("sl")
    last = ns - 1
    up = (lax.rem(x + nx - 1, nx), y, s_me)
    down = (lax.rem(x + 1, nx), y, s_me)
    left = (x, lax.rem(y + ny - 1, ny), s_me)
    right = (x, lax.rem(y + 1, ny), s_me)
    after = (x, y, jnp.minimum(s_me + 1, last))
    before = (x, y, jnp.maximum(s_me - 1, 0))
    top, bottom = pl.ds(0, half), pl.ds(half, half)

    barrier = pltpu.get_barrier_semaphore()
    for there in (up, down, left, right):
        pl.semaphore_signal(barrier, inc=1, device_id=there, device_id_type=MESH)

    @pl.when(s_me > 0)
    def _():
        pl.semaphore_signal(barrier, inc=1, device_id=before, device_id_type=MESH)

    @pl.when(s_me < last)
    def _():
        pl.semaphore_signal(barrier, inc=1, device_id=after, device_id_type=MESH)

    ends = jnp.where(s_me > 0, 1, 0) + jnp.where(s_me < last, 1, 0)
    pl.semaphore_wait(barrier, 4 + ends)

    def remote(src, dst, send, recv, there):
        return pltpu.make_async_remote_copy(
            src_ref=src,
            dst_ref=dst,
            send_sem=send,
            recv_sem=recv,
            device_id=there,
            device_id_type=MESH,
        )

    def pos_copies():
        return [
            remote(pos, posbuf.at[0], p_s.at[0], p_r.at[0], right),
            remote(pos, posbuf.at[1], p_s.at[1], p_r.at[1], left),
        ]

    def y_copies(s):
        return [
            remote(obj.at[s, :, top], ybuf.at[s, :, top], y_s.at[s, 0], y_r.at[s, 0], up),
            remote(obj.at[s, :, bottom], ybuf.at[s, :, bottom], y_s.at[s, 1], y_r.at[s, 1], down),
        ]

    def z_copies(s):
        return [
            remote(zs.at[s, 0], zr.at[s, 0], z_s.at[s, 0], z_r.at[s, 0], left),
            remote(zs.at[s, 1], zr.at[s, 1], z_s.at[s, 1], z_r.at[s, 1], right),
        ]

    def gz_copies(s):
        return [
            remote(gzs.at[s, 0], gzr.at[s, 0], gz_s.at[s, 0], gz_r.at[s, 0], right),
            remote(gzs.at[s, 1], gzr.at[s, 1], gz_s.at[s, 1], gz_r.at[s, 1], left),
        ]

    def gy_copies(s):
        return [
            remote(gys.at[s, :, top], gyr.at[s, :, top], gy_s.at[s, 0], gy_r.at[s, 0], down),
            remote(gys.at[s, :, bottom], gyr.at[s, :, bottom], gy_s.at[s, 1], gy_r.at[s, 1], up),
        ]

    def wave_copy():
        return remote(psi.at[layers], psi.at[0], w_s.at[0], w_r.at[0], after)

    def adj_copy():
        return remote(adj.at[0], adj.at[layers], w_s.at[1], w_r.at[1], before)

    for copy in pos_copies():
        copy.start()
    for s in range(layers):
        for copy in y_copies(s):
            copy.start()

    for which in range(2):
        for part in range(2):
            real = tab[which, 2 * part]
            imag = tab[which, 2 * part + 1]
            t_right[which, part, 0:width, 0:width] = real
            t_right[which, part, 0:width, width : 2 * width] = imag
            t_right[which, part, width : 2 * width, 0:width] = -imag
            t_right[which, part, width : 2 * width, width : 2 * width] = real
            t_left[which, part, 0:width, 0:width] = real
            t_left[which, part, 0:width, width : 2 * width] = -imag
            t_left[which, part, width : 2 * width, 0:width] = imag
            t_left[which, part, width : 2 * width, width : 2 * width] = real

    @pl.when(s_me == 0)
    def _():
        psi[0] = ill[...]

    def own_rows(row):
        cells = lax.broadcasted_iota(jnp.int32, (width, half), 0)
        return (cells >= row - half) & (cells < row + half)

    def own_cols(side):
        cells = lax.broadcasted_iota(jnp.int32, (width, half), 1) + side * half
        col = pos[1, 0:1, 0:half]
        return (cells >= col - half) & (cells < col + half)

    def my_rows():
        return own_rows(pos[0, 0:1, 0:half])

    def their_rows(slot):
        return own_rows(posbuf[slot, 0, 0:1, 0:half])

    sides = (slice(0, half), slice(half, width))

    for copy in pos_copies():
        copy.wait_recv()

    def send_columns(s, carry):
        for copy in y_copies(s):
            copy.wait_recv()
        for side in range(2):
            rows = their_rows(side)
            for part in range(2):
                zs[s, side, part] = jnp.where(
                    rows, obj[s, part, :, sides[side]], ybuf[s, part, :, sides[side]]
                )
        for copy in z_copies(s):
            copy.start()
        return carry

    lax.fori_loop(0, layers, send_columns, 0)

    def sandwich(which, real, imag):
        high, low = split(jnp.concatenate([real, imag], axis=0))
        t_h, t_l = t_left[which, 0], t_left[which, 1]
        done = dot(t_h, high) + dot(t_h, low) + dot(t_l, high)
        high, low = split(jnp.concatenate([done[:width], done[width:]], axis=1))
        t_h, t_l = t_right[which, 0], t_right[which, 1]
        done = dot(high, t_h) + dot(low, t_h) + dot(high, t_l)
        return done[:, :width], done[:, width:]

    def table_of(s):
        return jnp.where((s_me == last) & (s == layers - 1), 1, 0)

    def go_forward(s, carry):
        for copy in z_copies(s):
            copy.wait_recv()
        rows = my_rows()
        for side in range(2):
            cols = own_cols(side)
            for part in range(2):
                mixed = jnp.where(
                    rows, obj[s, part, :, sides[side]], ybuf[s, part, :, sides[side]]
                )
                win[s, part, :, sides[side]] = jnp.where(cols, mixed, zr[s, side, part])

        @pl.when((s == 0) & (s_me > 0))
        def _():
            wave_copy().wait_recv()

        w_re, w_im = win[s, 0], win[s, 1]
        p_re, p_im = psi[s, 0], psi[s, 1]
        o_re, o_im = sandwich(
            table_of(s), w_re * p_re - w_im * p_im, w_re * p_im + w_im * p_re
        )
        psi[s + 1, 0] = o_re
        psi[s + 1, 1] = o_im
        return carry

    lax.fori_loop(0, layers, go_forward, 0)

    @pl.when(s_me < last)
    def _():
        wave_copy().start()
        adj_copy().wait_recv()

    @pl.when(s_me == last)
    def _():
        f_re, f_im = psi[layers, 0], psi[layers, 1]
        residual = f_re * f_re + f_im * f_im - meas[...]
        adj[layers, 0] = residual * f_re
        adj[layers, 1] = residual * f_im

    def go_back(step, carry):
        s = layers - 1 - step
        i_re, minus_im = sandwich(table_of(s), adj[s + 1, 0], -adj[s + 1, 1])
        i_im = -minus_im
        w_re, w_im = win[s, 0], win[s, 1]
        adj[s, 0] = w_re * i_re + w_im * i_im
        adj[s, 1] = w_re * i_im - w_im * i_re

        @pl.when((s == 0) & (s_me > 0))
        def _():
            adj_copy().start()

        p_re, p_im = psi[s, 0], psi[s, 1]
        terms = (p_re * i_re + p_im * i_im, p_re * i_im - p_im * i_re)
        for side in range(2):
            cols = own_cols(side)
            for part in range(2):
                here = terms[part][:, sides[side]]
                gzs[s, side, part] = jnp.where(cols, 0.0, here)
                term[s, part, :, sides[side]] = jnp.where(cols, here, 0.0)
        for copy in gz_copies(s):
            copy.start()
        return carry

    lax.fori_loop(0, layers, go_back, 0)

    def send_rows(step, carry):
        s = layers - 1 - step
        for copy in gz_copies(s):
            copy.wait_recv()
        rows = my_rows()
        for side in range(2):
            theirs = their_rows(side)
            for part in range(2):
                mine = term[s, part, :, sides[side]]
                came = gzr[s, side, part]
                gys[s, part, :, sides[side]] = jnp.where(rows, 0.0, mine) + jnp.where(
                    theirs, 0.0, came
                )
                term[s, part, :, sides[side]] = jnp.where(rows, mine, 0.0) + jnp.where(
                    theirs, came, 0.0
                )
        for copy in gy_copies(s):
            copy.start()
        return carry

    lax.fori_loop(0, layers, send_rows, 0)

    def finish(step, carry):
        s = layers - 1 - step
        for copy in gy_copies(s):
            copy.wait_recv()
        out[s] = obj[s] - STEP_SIZE * (term[s] + gyr[s])
        return carry

    lax.fori_loop(0, layers, finish, 0)

    for copy in pos_copies():
        copy.wait_send()
    for s in range(layers):
        for copies in (y_copies, z_copies, gz_copies, gy_copies):
            for copy in copies(s):
                copy.wait_send()

    @pl.when(s_me < last)
    def _():
        wave_copy().wait_send()

    @pl.when(s_me > 0)
    def _():
        adj_copy().wait_send()


def body(object_field, illumination, positions, measured):
    layers = object_field.shape[0]
    width = illumination.shape[-1]
    half = width // 2
    counts = tuple(lax.axis_size(a) for a in ("tx", "ty", "sl"))
    offset = positions.reshape(2)
    rolled = jnp.roll(illumination, (offset[0] - half, offset[1] - half), axis=(1, 2))
    pos = jnp.broadcast_to(offset[:, None, None], (2, 8, half)).astype(jnp.int32)
    tables = jnp.asarray(build_tables(width))
    f32 = jnp.float32
    wave = (layers, 2, width, width)
    strips = (layers, 2, 2, width, half)
    pairs = pltpu.SemaphoreType.DMA((layers, 2))
    two = pltpu.SemaphoreType.DMA((2,))
    return pl.pallas_call(
        functools.partial(kernel, counts),
        out_shape=jax.ShapeDtypeStruct(object_field.shape, f32),
        in_specs=[pl.BlockSpec(memory_space=pltpu.VMEM)] * 5,
        out_specs=pl.BlockSpec(memory_space=pltpu.VMEM),
        scratch_shapes=[
            pltpu.VMEM((2, 2, 2 * width, 2 * width), jnp.bfloat16),
            pltpu.VMEM((2, 2, 2 * width, 2 * width), jnp.bfloat16),
            pltpu.VMEM(wave, f32),
            pltpu.VMEM(strips, f32),
            pltpu.VMEM(strips, f32),
            pltpu.VMEM(wave, f32),
            pltpu.VMEM((layers + 1, 2, width, width), f32),
            pltpu.VMEM((layers + 1, 2, width, width), f32),
            pltpu.VMEM(wave, f32),
            pltpu.VMEM(strips, f32),
            pltpu.VMEM(strips, f32),
            pltpu.VMEM(wave, f32),
            pltpu.VMEM(wave, f32),
            pltpu.VMEM((2, 2, 8, half), jnp.int32),
        ]
        + [pairs] * 8
        + [two] * 4,
        compiler_params=pltpu.CompilerParams(
            collective_id=0, has_side_effects=True, vmem_limit_bytes=48 * 1024 * 1024
        ),
    )(object_field, rolled, pos, measured.reshape(width, width), tables)


def solution(mesh):
    placed = (
        P("sl", None, "tx", "ty"),
        P(),
        P("tx", "ty", None, None),
        P("tx", "ty", None, None, None),
    )
    return jax.shard_map(
        body, mesh=mesh, in_specs=placed, out_specs=P("sl", None, "tx", "ty"), check_vma=False
    )
```

time: 475 us -> 129 us (0.27); the launches traced: 469 us -> 129 us
  waiting for transfers between devices: 298 us -> 0 us
  Pallas kernels: 0 us -> 122 us
  starting transfers between devices: 49.5 us -> 0 us
  loops' own time: 48.8 us -> 0 us
  local copies, waits for them, and re-layouts: 34.8 us -> 3.27 us
  matrix products: 23.8 us -> 0 us
  other arithmetic: 14 us -> 1.68 us
    ppermute x14 -> x0, waiting for transfers between devices: 298 us -> none  [the longest x6 199 us: shifted_2(): return lax.ppermute(x, axis, pairs)]
    pallas_call x0 -> x1, Pallas kernels: none -> 122 us  [body(): pl.pallas_call(functools.partial(kernel, counts), out_shape=jax.ShapeDtyp...]
    ppermute x14 -> x0, starting transfers between devices: 49.5 us -> none  [the longest x6 38.5 us: shifted_2(): return lax.ppermute(x, axis, pairs)]
    another operation x9 -> x0, loops' own time: 48.8 us -> none  [the longest x4 40.4 us: body(): lax.cond(active, run_forward, skip_forward, (source, saved_all, exit_grads))]
    dot_general x36 -> x0, matrix products: 23.8 us -> none  [the longest x16 12 us: product(): jnp.einsum('bjk,kl->bjl', left_matrix, right_matrix, precision=PRECISE)]
    dynamic_update_slice x2 -> x0, local copies, waits for them, and re-layouts: 13.5 us -> none  [section_backward(): lax.dynamic_update_slice(gradient_sum, current + contrib[0][None], corner...]
    slice x8 -> x1, local copies, waits for them, and re-layouts: 9.27 us -> 0.59 us  [body(): offset[0] - half]
    add x4 -> x0, other arithmetic: 6.15 us -> none  [the longest x2 2.74 us: section_backward(): current + contrib[0][None]]
  transfers between devices with their start and end apart: 14 -> 0, of which waited for: 14 -> 0; matrix products, arithmetic and copies ran while one was open for 2% -> 0% of each run, Pallas kernels for 0% -> 0%
where the time goes in v1:
time: 129 us
  Pallas kernels  122 us (95%)
  local copies, waits for them, and re-layouts  3.27 us (3%)
  other arithmetic  1.68 us (1%)
  between operations  1.34 us (1%)
    pallas_call x1, Pallas kernels, body(): pl.pallas_call(functools.partial(kernel, counts), out_shape=jax.ShapeDtyp...  122 us
    unnamed x9, local copies, waits for them, and re-layouts  2.61 us

profile of v1, /device:TPU:0, one launch (start us, length us, event | category | flops | bytes accessed | tf_op | source)
XLA Modules:
  0.0 128.6 jit_solution(2944064827698835247)
XLA Ops:
  0.0 0.0 copy-start.3
  0.0 0.7 copy-done.3
  0.7 0.6 fusion.2
  2.6 0.1 broadcast_in_dim.10.pos
  2.6 0.0 copy-start
  2.6 0.0 copy-start.1
  2.6 1.3 %fusion.1 = f32[2,256,256]{2,1,0:T(8,128)S(1)} fusion(s32[]{:T(128)S(6)} %select_n.24, f32[2,256,256]{2,1,0:T(8,128)} %param.6), kind=kLoop, calls=%fused_computation.5 | loop fusion | flops 131072 | bytes 1048580 | tf_op jit(solution)/shard_map/jit(_roll_dynamic)/concatenate | solution.py:347
  4.0 0.3 fusion.ill
  4.3 0.0 copy-done
  4.3 0.0 copy-done.1
  4.4 0.0 copy-start.2
  4.4 0.9 copy-done.2
  5.3 122.3 %shard_map.55 = f32[2,2,256,256]{3,2,1,0:T(8,128)S(1)} custom-call(f32[2,2,256,256]{3,2,1,0:T(8,128)S(1)} %copy-done, f32[2,256,256]{2,1,0:T(8,128)S(1)} %fusion.ill, s32[2,8,128]{2,1,0:T(8,128)S(1)} %broadcast_in_dim.10.pos, f32[256,256]{1,0:T(8,128)S(1)} %bitcast.4, bf16[2,4,256,256]{3,2,1,0:T(8,128)(2,1)S(1)} %copy-done.1), custom_call_target="tpu_custom_call" | custom-call | tf_op jit(solution)/shard_map/pallas_call | solution.py:355
  127.6 1.0 copy.7
Async XLA Ops:
  0.0 0.7 copy-start.3
  2.6 1.7 %copy-start = (f32[2,2,256,256]{3,2,1,0:T(8,128)S(1)}, f32[2,2,256,256]{3,2,1,0:T(8,128)}, u32[]{:S(2)}) copy-start(f32[2,2,256,256]{3,2,1,0:T(8,128)} %obj.1) | copy-start | bytes 3145732
  2.6 1.7 %copy-start.1 = (bf16[2,4,256,256]{3,2,1,0:T(8,128)(2,1)S(1)}, bf16[2,4,256,256]{3,2,1,0:T(8,128)(2,1)}, u32[]{:S(2)}) copy-start(bf16[2,4,256,256]{3,2,1,0:T(8,128)(2,1)} %constant.37.clone.tab) | copy-start | bytes 3145732
  4.4 0.9 copy-start.2

commit v2 on v1

--- a/solution.py
+++ b/solution.py
@@ -126,28 +126,30 @@
             remote(pos, posbuf.at[1], p_s.at[1], p_r.at[1], left),
         ]
 
-    def y_copies(s):
+    def y_copies(s, c):
+        a, b = obj.at[s, c], ybuf.at[s, c]
         return [
-            remote(obj.at[s, :, top], ybuf.at[s, :, top], y_s.at[s, 0], y_r.at[s, 0], up),
-            remote(obj.at[s, :, bottom], ybuf.at[s, :, bottom], y_s.at[s, 1], y_r.at[s, 1], down),
-        ]
-
-    def z_copies(s):
+            remote(a.at[top], b.at[top], y_s.at[s, c, 0], y_r.at[s, c, 0], up),
+            remote(a.at[bottom], b.at[bottom], y_s.at[s, c, 1], y_r.at[s, c, 1], down),
+        ]
+
+    def z_copies(s, c):
         return [
-            remote(zs.at[s, 0], zr.at[s, 0], z_s.at[s, 0], z_r.at[s, 0], left),
-            remote(zs.at[s, 1], zr.at[s, 1], z_s.at[s, 1], z_r.at[s, 1], right),
-        ]
-
-    def gz_copies(s):
+            remote(zs.at[s, 0, c], zr.at[s, 0, c], z_s.at[s, c, 0], z_r.at[s, c, 0], left),
+            remote(zs.at[s, 1, c], zr.at[s, 1, c], z_s.at[s, c, 1], z_r.at[s, c, 1], right),
+        ]
+
+    def gz_copies(s, c):
         return [
-            remote(gzs.at[s, 0], gzr.at[s, 0], gz_s.at[s, 0], gz_r.at[s, 0], right),
-            remote(gzs.at[s, 1], gzr.at[s, 1], gz_s.at[s, 1], gz_r.at[s, 1], left),
-        ]
-
-    def gy_copies(s):
+            remote(gzs.at[s, 0, c], gzr.at[s, 0, c], gz_s.at[s, c, 0], gz_r.at[s, c, 0], right),
+            remote(gzs.at[s, 1, c], gzr.at[s, 1, c], gz_s.at[s, c, 1], gz_r.at[s, c, 1], left),
+        ]
+
+    def gy_copies(s, c):
+        a, b = gys.at[s, c], gyr.at[s, c]
         return [
-            remote(gys.at[s, :, top], gyr.at[s, :, top], gy_s.at[s, 0], gy_r.at[s, 0], down),
-            remote(gys.at[s, :, bottom], gyr.at[s, :, bottom], gy_s.at[s, 1], gy_r.at[s, 1], up),
+            remote(a.at[top], b.at[top], gy_s.at[s, c, 0], gy_r.at[s, c, 0], down),
+            remote(a.at[bottom], b.at[bottom], gy_s.at[s, c, 1], gy_r.at[s, c, 1], up),
         ]
 
     def wave_copy():
@@ -159,8 +161,9 @@
     for copy in pos_copies():
         copy.start()
     for s in range(layers):
-        for copy in y_copies(s):
-            copy.start()
+        for c in range(2):
+            for copy in y_copies(s, c):
+                copy.start()
 
     for which in range(2):
         for part in range(2):
@@ -170,10 +173,12 @@
             t_right[which, part, 0:width, width : 2 * width] = imag
             t_right[which, part, width : 2 * width, 0:width] = -imag
             t_right[which, part, width : 2 * width, width : 2 * width] = real
-            t_left[which, part, 0:width, 0:width] = real
-            t_left[which, part, 0:width, width : 2 * width] = -imag
-            t_left[which, part, width : 2 * width, 0:width] = imag
-            t_left[which, part, width : 2 * width, width : 2 * width] = real
+            first = slice(2 * part * width, (2 * part + 1) * width)
+            second = slice((2 * part + 1) * width, (2 * part + 2) * width)
+            t_left[which, first, 0:width] = real
+            t_left[which, first, width : 2 * width] = -imag
+            t_left[which, second, 0:width] = imag
+            t_left[which, second, width : 2 * width] = real
 
     @pl.when(s_me == 0)
     def _():
@@ -200,35 +205,38 @@
         copy.wait_recv()
 
     def send_columns(s, carry):
-        for copy in y_copies(s):
-            copy.wait_recv()
-        for side in range(2):
-            rows = their_rows(side)
-            for part in range(2):
+        for part in range(2):
+            for copy in y_copies(s, part):
+                copy.wait_recv()
+            for side in range(2):
                 zs[s, side, part] = jnp.where(
-                    rows, obj[s, part, :, sides[side]], ybuf[s, part, :, sides[side]]
+                    their_rows(side),
+                    obj[s, part, :, sides[side]],
+                    ybuf[s, part, :, sides[side]],
                 )
-        for copy in z_copies(s):
-            copy.start()
+            for copy in z_copies(s, part):
+                copy.start()
         return carry
 
     lax.fori_loop(0, layers, send_columns, 0)
 
     def sandwich(which, real, imag):
+        wide = 2 * width
         high, low = split(jnp.concatenate([real, imag], axis=0))
-        t_h, t_l = t_left[which, 0], t_left[which, 1]
-        done = dot(t_h, high) + dot(t_h, low) + dot(t_l, high)
+        two = dot(t_left[which], high)
+        done = two[:wide] + two[wide:] + dot(t_left[which, 0:wide], low)
         high, low = split(jnp.concatenate([done[:width], done[width:]], axis=1))
-        t_h, t_l = t_right[which, 0], t_right[which, 1]
-        done = dot(high, t_h) + dot(low, t_h) + dot(high, t_l)
+        two = dot(jnp.concatenate([high, low], axis=0), t_right[which, 0])
+        done = two[:width] + two[width:] + dot(high, t_right[which, 1])
         return done[:, :width], done[:, width:]
 
     def table_of(s):
         return jnp.where((s_me == last) & (s == layers - 1), 1, 0)
 
     def go_forward(s, carry):
-        for copy in z_copies(s):
-            copy.wait_recv()
+        for c in range(2):
+            for copy in z_copies(s, c):
+                copy.wait_recv()
         rows = my_rows()
         for side in range(2):
             cols = own_cols(side)
@@ -279,26 +287,26 @@
 
         p_re, p_im = psi[s, 0], psi[s, 1]
         terms = (p_re * i_re + p_im * i_im, p_re * i_im - p_im * i_re)
-        for side in range(2):
-            cols = own_cols(side)
-            for part in range(2):
+        for part in range(2):
+            for side in range(2):
+                cols = own_cols(side)
                 here = terms[part][:, sides[side]]
                 gzs[s, side, part] = jnp.where(cols, 0.0, here)
                 term[s, part, :, sides[side]] = jnp.where(cols, here, 0.0)
-        for copy in gz_copies(s):
-            copy.start()
+            for copy in gz_copies(s, part):
+                copy.start()
         return carry
 
     lax.fori_loop(0, layers, go_back, 0)
 
     def send_rows(step, carry):
         s = layers - 1 - step
-        for copy in gz_copies(s):
-            copy.wait_recv()
-        rows = my_rows()
-        for side in range(2):
-            theirs = their_rows(side)
-            for part in range(2):
+        for part in range(2):
+            for copy in gz_copies(s, part):
+                copy.wait_recv()
+            rows = my_rows()
+            for side in range(2):
+                theirs = their_rows(side)
                 mine = term[s, part, :, sides[side]]
                 came = gzr[s, side, part]
                 gys[s, part, :, sides[side]] = jnp.where(rows, 0.0, mine) + jnp.where(
@@ -307,17 +315,18 @@
                 term[s, part, :, sides[side]] = jnp.where(rows, mine, 0.0) + jnp.where(
                     theirs, came, 0.0
                 )
-        for copy in gy_copies(s):
-            copy.start()
+            for copy in gy_copies(s, part):
+                copy.start()
         return carry
 
     lax.fori_loop(0, layers, send_rows, 0)
 
     def finish(step, carry):
         s = layers - 1 - step
-        for copy in gy_copies(s):
-            copy.wait_recv()
-        out[s] = obj[s] - STEP_SIZE * (term[s] + gyr[s])
+        for c in range(2):
+            for copy in gy_copies(s, c):
+                copy.wait_recv()
+            out[s, c] = obj[s, c] - STEP_SIZE * (term[s, c] + gyr[s, c])
         return carry
 
     lax.fori_loop(0, layers, finish, 0)
@@ -326,7 +335,7 @@
         copy.wait_send()
     for s in range(layers):
         for copies in (y_copies, z_copies, gz_copies, gy_copies):
-            for copy in copies(s):
+            for copy in copies(s, 0) + copies(s, 1):
                 copy.wait_send()
 
     @pl.when(s_me < last)
@@ -350,7 +359,7 @@
     f32 = jnp.float32
     wave = (layers, 2, width, width)
     strips = (layers, 2, 2, width, half)
-    pairs = pltpu.SemaphoreType.DMA((layers, 2))
+    pairs = pltpu.SemaphoreType.DMA((layers, 2, 2))
     two = pltpu.SemaphoreType.DMA((2,))
     return pl.pallas_call(
         functools.partial(kernel, counts),
@@ -358,7 +367,7 @@
         in_specs=[pl.BlockSpec(memory_space=pltpu.VMEM)] * 5,
         out_specs=pl.BlockSpec(memory_space=pltpu.VMEM),
         scratch_shapes=[
-            pltpu.VMEM((2, 2, 2 * width, 2 * width), jnp.bfloat16),
+            pltpu.VMEM((2, 4 * width, 2 * width), jnp.bfloat16),
             pltpu.VMEM((2, 2, 2 * width, 2 * width), jnp.bfloat16),
             pltpu.VMEM(wave, f32),
             pltpu.VMEM(strips, f32),

time: 129 us -> 118 us (0.915)
  Pallas kernels: 122 us -> 111 us
    pallas_call x1, Pallas kernels: 122 us -> 111 us  [body(): pl.pallas_call(functools.partial(kernel, counts), out_shape=jax.ShapeDtyp...]
where the time goes in v2:
time: 118 us; the launch traced here: 117 us
  Pallas kernels  111 us (94%)
  local copies, waits for them, and re-layouts  3.24 us (3%)
  other arithmetic  1.69 us (1%)
  between operations  1.35 us (1%)
    pallas_call x1, Pallas kernels, body(): pl.pallas_call(functools.partial(kernel, counts), out_shape=jax.ShapeDtyp...  111 us
    unnamed x9, local copies, waits for them, and re-layouts  2.58 us

profile of v2, /device:TPU:0, one launch (start us, length us, event | category | flops | bytes accessed | tf_op | source)
XLA Modules:
  0.0 117.5 jit_solution(15231212766993090267)
XLA Ops:
  0.0 0.0 copy-start.3
  0.0 0.7 copy-done.3
  0.7 0.6 fusion.2
  2.6 0.1 broadcast_in_dim.10.pos
  2.6 0.0 copy-start
  2.6 0.0 copy-start.1
  2.6 1.3 %fusion.1 = f32[2,256,256]{2,1,0:T(8,128)S(1)} fusion(s32[]{:T(128)S(6)} %select_n.24, f32[2,256,256]{2,1,0:T(8,128)} %param.6), kind=kLoop, calls=%fused_computation.5 | loop fusion | flops 131072 | bytes 1048580 | tf_op jit(solution)/shard_map/jit(_roll_dynamic)/concatenate | solution.py:356
  4.0 0.3 fusion.ill
  4.3 0.0 copy-done
  4.3 0.0 copy-done.1
  4.3 0.0 copy-start.2
  4.4 0.9 copy-done.2
  5.3 111.2 %shard_map.55 = f32[2,2,256,256]{3,2,1,0:T(8,128)S(1)} custom-call(f32[2,2,256,256]{3,2,1,0:T(8,128)S(1)} %copy-done, f32[2,256,256]{2,1,0:T(8,128)S(1)} %fusion.ill, s32[2,8,128]{2,1,0:T(8,128)S(1)} %broadcast_in_dim.10.pos, f32[256,256]{1,0:T(8,128)S(1)} %bitcast.4, bf16[2,4,256,256]{3,2,1,0:T(8,128)(2,1)S(1)} %copy-done.1), custom_call_target="tpu_custom_call" | custom-call | tf_op jit(solution)/shard_map/pallas_call | solution.py:364
  116.5 1.0 copy.7
Async XLA Ops:
  0.0 0.7 copy-start.3
  2.6 1.7 %copy-start = (f32[2,2,256,256]{3,2,1,0:T(8,128)S(1)}, f32[2,2,256,256]{3,2,1,0:T(8,128)}, u32[]{:S(2)}) copy-start(f32[2,2,256,256]{3,2,1,0:T(8,128)} %obj.1) | copy-start | bytes 3145732
  2.6 1.7 %copy-start.1 = (bf16[2,4,256,256]{3,2,1,0:T(8,128)(2,1)S(1)}, bf16[2,4,256,256]{3,2,1,0:T(8,128)(2,1)}, u32[]{:S(2)}) copy-start(bf16[2,4,256,256]{3,2,1,0:T(8,128)(2,1)} %constant.37.clone.tab) | copy-start | bytes 3145732
  4.3 1.0 copy-start.2

commit v3 on v2

--- a/solution.py
+++ b/solution.py
@@ -76,8 +76,12 @@
     gy_r,
     p_s,
     p_r,
-    w_s,
-    w_r,
+    x_s,
+    x_r,
+    m_s,
+    m_r,
+    n_s,
+    n_r,
 ):
     nx, ny, ns = counts
     layers = obj.shape[0]
@@ -91,24 +95,29 @@
     down = (lax.rem(x + 1, nx), y, s_me)
     left = (x, lax.rem(y + ny - 1, ny), s_me)
     right = (x, lax.rem(y + 1, ny), s_me)
-    after = (x, y, jnp.minimum(s_me + 1, last))
-    before = (x, y, jnp.maximum(s_me - 1, 0))
+    pair, core = lax.div(s_me, 2), lax.rem(s_me, 2)
+    last_pair = ns // 2 - 1
+    depth = 2 * layers
+    mate = (x, y, s_me + 1 - 2 * core)
+    after = (x, y, jnp.minimum(s_me + 2, last))
+    before = (x, y, jnp.maximum(s_me - 2, 0))
+    my_half = pl.ds(pl.multiple_of(core * half, half), half)
     top, bottom = pl.ds(0, half), pl.ds(half, half)
 
     barrier = pltpu.get_barrier_semaphore()
-    for there in (up, down, left, right):
+    for there in (up, down, left, right, mate):
         pl.semaphore_signal(barrier, inc=1, device_id=there, device_id_type=MESH)
 
-    @pl.when(s_me > 0)
+    @pl.when(pair > 0)
     def _():
         pl.semaphore_signal(barrier, inc=1, device_id=before, device_id_type=MESH)
 
-    @pl.when(s_me < last)
+    @pl.when(pair < last_pair)
     def _():
         pl.semaphore_signal(barrier, inc=1, device_id=after, device_id_type=MESH)
 
-    ends = jnp.where(s_me > 0, 1, 0) + jnp.where(s_me < last, 1, 0)
-    pl.semaphore_wait(barrier, 4 + ends)
+    ends = jnp.where(pair > 0, 1, 0) + jnp.where(pair < last_pair, 1, 0)
+    pl.semaphore_wait(barrier, 5 + ends)
 
     def remote(src, dst, send, recv, there):
         return pltpu.make_async_remote_copy(
@@ -152,11 +161,32 @@
             remote(a.at[bottom], b.at[bottom], gy_s.at[s, c, 1], gy_r.at[s, c, 1], up),
         ]
 
-    def wave_copy():
-        return remote(psi.at[layers], psi.at[0], w_s.at[0], w_r.at[0], after)
-
-    def adj_copy():
-        return remote(adj.at[0], adj.at[layers], w_s.at[1], w_r.at[1], before)
+    def window_copy(s):
+        at = core * layers + s
+        return remote(win.at[at], win.at[at], n_s.at[s], n_r.at[s], mate)
+
+    def wave_copy(c):
+        src, dst = psi.at[depth, c, my_half], psi.at[0, c, my_half]
+        return remote(src, dst, x_s.at[0, c], x_r.at[0, c], after)
+
+    def wave_share(c):
+        block = psi.at[0, c, my_half]
+        return remote(block, block, m_s.at[0, c], m_r.at[0, c], mate)
+
+    def adj_copy(c):
+        src, dst = adj.at[0, c, my_half], adj.at[depth, c, my_half]
+        return remote(src, dst, x_s.at[1, c], x_r.at[1, c], before)
+
+    def adj_share(c):
+        block = adj.at[depth, c, my_half]
+        return remote(block, block, m_s.at[1, c], m_r.at[1, c], mate)
+
+    def receive(copy, share):
+        for c in range(2):
+            copy(c).wait_recv()
+            share(c).start()
+        for c in range(2):
+            share(c).wait_recv()
 
     for copy in pos_copies():
         copy.start()
@@ -180,7 +210,7 @@
             t_left[which, second, 0:width] = imag
             t_left[which, second, width : 2 * width] = real
 
-    @pl.when(s_me == 0)
+    @pl.when(pair == 0)
     def _():
         psi[0] = ill[...]
 
@@ -230,74 +260,97 @@
         done = two[:width] + two[width:] + dot(high, t_right[which, 1])
         return done[:, :width], done[:, width:]
 
-    def table_of(s):
-        return jnp.where((s_me == last) & (s == layers - 1), 1, 0)
-
-    def go_forward(s, carry):
+    def table_of(g):
+        return jnp.where((pair == last_pair) & (g == depth - 1), 1, 0)
+
+    def go_forward(g, carry):
+        owner = lax.div(g, layers)
+
+        @pl.when(owner != core)
+        def _():
+            window_copy(g - owner * layers).wait_recv()
+
+        w_re, w_im = win[g, 0], win[g, 1]
+        p_re, p_im = psi[g, 0], psi[g, 1]
+        o_re, o_im = sandwich(
+            table_of(g), w_re * p_re - w_im * p_im, w_re * p_im + w_im * p_re
+        )
+        psi[g + 1, 0] = o_re
+        psi[g + 1, 1] = o_im
+        return carry
+
+    def build_window(s, carry):
         for c in range(2):
             for copy in z_copies(s, c):
                 copy.wait_recv()
         rows = my_rows()
+        at = core * layers + s
         for side in range(2):
             cols = own_cols(side)
             for part in range(2):
                 mixed = jnp.where(
                     rows, obj[s, part, :, sides[side]], ybuf[s, part, :, sides[side]]
                 )
-                win[s, part, :, sides[side]] = jnp.where(cols, mixed, zr[s, side, part])
-
-        @pl.when((s == 0) & (s_me > 0))
+                win[at, part, :, sides[side]] = jnp.where(cols, mixed, zr[s, side, part])
+        window_copy(s).start()
+
+        @pl.when(pair == 0)
         def _():
-            wave_copy().wait_recv()
-
-        w_re, w_im = win[s, 0], win[s, 1]
-        p_re, p_im = psi[s, 0], psi[s, 1]
-        o_re, o_im = sandwich(
-            table_of(s), w_re * p_re - w_im * p_im, w_re * p_im + w_im * p_re
-        )
-        psi[s + 1, 0] = o_re
-        psi[s + 1, 1] = o_im
-        return carry
-
-    lax.fori_loop(0, layers, go_forward, 0)
-
-    @pl.when(s_me < last)
-    def _():
-        wave_copy().start()
-        adj_copy().wait_recv()
-
-    @pl.when(s_me == last)
-    def _():
-        f_re, f_im = psi[layers, 0], psi[layers, 1]
+            go_forward(s, 0)
+
+        return carry
+
+    lax.fori_loop(0, layers, build_window, 0)
+
+    @pl.when(pair > 0)
+    def _():
+        receive(wave_copy, wave_share)
+
+    lax.fori_loop(jnp.where(pair == 0, layers, 0), depth, go_forward, 0)
+
+    @pl.when(pair < last_pair)
+    def _():
+        for c in range(2):
+            wave_copy(c).start()
+        receive(adj_copy, adj_share)
+
+    @pl.when(pair == last_pair)
+    def _():
+        f_re, f_im = psi[depth, 0], psi[depth, 1]
         residual = f_re * f_re + f_im * f_im - meas[...]
-        adj[layers, 0] = residual * f_re
-        adj[layers, 1] = residual * f_im
+        adj[depth, 0] = residual * f_re
+        adj[depth, 1] = residual * f_im
 
     def go_back(step, carry):
-        s = layers - 1 - step
-        i_re, minus_im = sandwich(table_of(s), adj[s + 1, 0], -adj[s + 1, 1])
+        g = depth - 1 - step
+        i_re, minus_im = sandwich(table_of(g), adj[g + 1, 0], -adj[g + 1, 1])
         i_im = -minus_im
-        w_re, w_im = win[s, 0], win[s, 1]
-        adj[s, 0] = w_re * i_re + w_im * i_im
-        adj[s, 1] = w_re * i_im - w_im * i_re
-
-        @pl.when((s == 0) & (s_me > 0))
+        w_re, w_im = win[g, 0], win[g, 1]
+        adj[g, 0] = w_re * i_re + w_im * i_im
+        adj[g, 1] = w_re * i_im - w_im * i_re
+
+        @pl.when((g == 0) & (pair > 0))
         def _():
-            adj_copy().start()
-
-        p_re, p_im = psi[s, 0], psi[s, 1]
-        terms = (p_re * i_re + p_im * i_im, p_re * i_im - p_im * i_re)
-        for part in range(2):
-            for side in range(2):
-                cols = own_cols(side)
-                here = terms[part][:, sides[side]]
-                gzs[s, side, part] = jnp.where(cols, 0.0, here)
-                term[s, part, :, sides[side]] = jnp.where(cols, here, 0.0)
-            for copy in gz_copies(s, part):
-                copy.start()
-        return carry
-
-    lax.fori_loop(0, layers, go_back, 0)
+            for c in range(2):
+                adj_copy(c).start()
+
+        @pl.when(lax.div(g, layers) == core)
+        def _():
+            s = g - core * layers
+            p_re, p_im = psi[g, 0], psi[g, 1]
+            terms = (p_re * i_re + p_im * i_im, p_re * i_im - p_im * i_re)
+            for part in range(2):
+                for side in range(2):
+                    cols = own_cols(side)
+                    here = terms[part][:, sides[side]]
+                    gzs[s, side, part] = jnp.where(cols, 0.0, here)
+                    term[s, part, :, sides[side]] = jnp.where(cols, here, 0.0)
+                for copy in gz_copies(s, part):
+                    copy.start()
+
+        return carry
+
+    lax.fori_loop(0, jnp.where((pair == 0) & (core == 1), layers, depth), go_back, 0)
 
     def send_rows(step, carry):
         s = layers - 1 - step
@@ -338,13 +391,19 @@
             for copy in copies(s, 0) + copies(s, 1):
                 copy.wait_send()
 
-    @pl.when(s_me < last)
-    def _():
-        wave_copy().wait_send()
-
-    @pl.when(s_me > 0)
-    def _():
-        adj_copy().wait_send()
+        window_copy(s).wait_send()
+
+    @pl.when(pair < last_pair)
+    def _():
+        for c in range(2):
+            wave_copy(c).wait_send()
+            adj_share(c).wait_send()
+
+    @pl.when(pair > 0)
+    def _():
+        for c in range(2):
+            adj_copy(c).wait_send()
+            wave_share(c).wait_send()
 
 
 def body(object_field, illumination, positions, measured):
@@ -361,6 +420,8 @@
     strips = (layers, 2, 2, width, half)
     pairs = pltpu.SemaphoreType.DMA((layers, 2, 2))
     two = pltpu.SemaphoreType.DMA((2,))
+    square = pltpu.SemaphoreType.DMA((2, 2))
+    windows = pltpu.SemaphoreType.DMA((layers,))
     return pl.pallas_call(
         functools.partial(kernel, counts),
         out_shape=jax.ShapeDtypeStruct(object_field.shape, f32),
@@ -372,9 +433,9 @@
             pltpu.VMEM(wave, f32),
             pltpu.VMEM(strips, f32),
             pltpu.VMEM(strips, f32),
-            pltpu.VMEM(wave, f32),
-            pltpu.VMEM((layers + 1, 2, width, width), f32),
-            pltpu.VMEM((layers + 1, 2, width, width), f32),
+            pltpu.VMEM((2 * layers, 2, width, width), f32),
+            pltpu.VMEM((2 * layers + 1, 2, width, width), f32),
+            pltpu.VMEM((2 * layers + 1, 2, width, width), f32),
             pltpu.VMEM(wave, f32),
             pltpu.VMEM(strips, f32),
             pltpu.VMEM(strips, f32),
@@ -383,7 +444,9 @@
             pltpu.VMEM((2, 2, 8, half), jnp.int32),
         ]
         + [pairs] * 8
-        + [two] * 4,
+        + [two] * 2
+        + [square] * 4
+        + [windows] * 2,
         compiler_params=pltpu.CompilerParams(
             collective_id=0, has_side_effects=True, vmem_limit_bytes=48 * 1024 * 1024
         ),

time: 118 us -> 114 us (0.966)
  Pallas kernels: 111 us -> 107 us
    pallas_call x1, Pallas kernels: 111 us -> 107 us  [body(): pl.pallas_call(functools.partial(kernel, counts), out_shape=jax.ShapeDtyp...]
where the time goes in v3:
time: 114 us
  Pallas kernels  107 us (94%)
  local copies, waits for them, and re-layouts  3.24 us (3%)
  other arithmetic  1.71 us (2%)
  between operations  1.36 us (1%)
    pallas_call x1, Pallas kernels, body(): pl.pallas_call(functools.partial(kernel, counts), out_shape=jax.ShapeDtyp...  107 us
    unnamed x9, local copies, waits for them, and re-layouts  2.58 us

profile of v3, /device:TPU:0, one launch (start us, length us, event | category | flops | bytes accessed | tf_op | source)
XLA Modules:
  0.0 113.6 jit_solution(260635924040763945)
XLA Ops:
  0.0 0.0 copy-start.3
  0.0 0.7 copy-done.3
  0.7 0.6 fusion.2
  2.6 0.1 broadcast_in_dim.10.pos
  2.6 0.0 copy-start
  2.6 0.0 copy-start.1
  2.6 1.4 %fusion.1 = f32[2,256,256]{2,1,0:T(8,128)S(1)} fusion(s32[]{:T(128)S(6)} %select_n.24, f32[2,256,256]{2,1,0:T(8,128)} %param.6), kind=kLoop, calls=%fused_computation.5 | loop fusion | flops 131072 | bytes 1048580 | tf_op jit(solution)/shard_map/jit(_roll_dynamic)/concatenate | solution.py:415
  4.0 0.4 fusion.ill
  4.4 0.0 copy-done
  4.4 0.0 copy-done.1
  4.4 0.0 copy-start.2
  4.4 0.9 copy-done.2
  5.3 107.3 %shard_map.55 = f32[2,2,256,256]{3,2,1,0:T(8,128)S(1)} custom-call(f32[2,2,256,256]{3,2,1,0:T(8,128)S(1)} %copy-done, f32[2,256,256]{2,1,0:T(8,128)S(1)} %fusion.ill, s32[2,8,128]{2,1,0:T(8,128)S(1)} %broadcast_in_dim.10.pos, f32[256,256]{1,0:T(8,128)S(1)} %bitcast.4, bf16[2,4,256,256]{3,2,1,0:T(8,128)(2,1)S(1)} %copy-done.1), custom_call_target="tpu_custom_call" | custom-call | tf_op jit(solution)/shard_map/pallas_call | solution.py:425
  112.6 1.0 copy.7
Async XLA Ops:
  0.0 0.7 copy-start.3
  2.6 1.7 %copy-start = (f32[2,2,256,256]{3,2,1,0:T(8,128)S(1)}, f32[2,2,256,256]{3,2,1,0:T(8,128)}, u32[]{:S(2)}) copy-start(f32[2,2,256,256]{3,2,1,0:T(8,128)} %obj.1) | copy-start | bytes 3145732
  2.6 1.7 %copy-start.1 = (bf16[2,4,256,256]{3,2,1,0:T(8,128)(2,1)S(1)}, bf16[2,4,256,256]{3,2,1,0:T(8,128)(2,1)}, u32[]{:S(2)}) copy-start(bf16[2,4,256,256]{3,2,1,0:T(8,128)(2,1)} %constant.37.clone.tab) | copy-start | bytes 3145732
  4.4 1.0 copy-start.2

commit v4 on v3

--- a/solution.py
+++ b/solution.py
@@ -46,12 +46,14 @@
 
 def kernel(
     counts,
-    obj,
+    obj_in,
     ill,
     pos,
     meas,
+    tab_in,
+    out,
+    obj,
     tab,
-    out,
     t_left,
     t_right,
     ybuf,
@@ -82,8 +84,13 @@
     m_r,
     n_s,
     n_r,
+    here_s,
 ):
     nx, ny, ns = counts
+    obj_copy = pltpu.make_async_copy(obj_in, obj, here_s.at[0])
+    tab_copy = pltpu.make_async_copy(tab_in, tab, here_s.at[1])
+    obj_copy.start()
+    tab_copy.start()
     layers = obj.shape[0]
     width = obj.shape[-1]
     half = width // 2
@@ -136,22 +143,36 @@
         ]
 
     def y_copies(s, c):
-        a, b = obj.at[s, c], ybuf.at[s, c]
+        a, b = obj_in.at[s, c], ybuf.at[s, c]
         return [
             remote(a.at[top], b.at[top], y_s.at[s, c, 0], y_r.at[s, c, 0], up),
             remote(a.at[bottom], b.at[bottom], y_s.at[s, c, 1], y_r.at[s, c, 1], down),
         ]
 
-    def z_copies(s, c):
+    def z_copies(s, c, h):
+        rows = (top, bottom)[h]
         return [
-            remote(zs.at[s, 0, c], zr.at[s, 0, c], z_s.at[s, c, 0], z_r.at[s, c, 0], left),
-            remote(zs.at[s, 1, c], zr.at[s, 1, c], z_s.at[s, c, 1], z_r.at[s, c, 1], right),
+            remote(
+                zs.at[s, side, c, rows],
+                zr.at[s, side, c, rows],
+                z_s.at[s, c, h, side],
+                z_r.at[s, c, h, side],
+                (left, right)[side],
+            )
+            for side in range(2)
         ]
 
-    def gz_copies(s, c):
+    def gz_copies(s, c, h):
+        rows = (top, bottom)[h]
         return [
-            remote(gzs.at[s, 0, c], gzr.at[s, 0, c], gz_s.at[s, c, 0], gz_r.at[s, c, 0], right),
-            remote(gzs.at[s, 1, c], gzr.at[s, 1, c], gz_s.at[s, c, 1], gz_r.at[s, c, 1], left),
+            remote(
+                gzs.at[s, side, c, rows],
+                gzr.at[s, side, c, rows],
+                gz_s.at[s, c, h, side],
+                gz_r.at[s, c, h, side],
+                (right, left)[side],
+            )
+            for side in range(2)
         ]
 
     def gy_copies(s, c):
@@ -195,6 +216,7 @@
             for copy in y_copies(s, c):
                 copy.start()
 
+    tab_copy.wait()
     for which in range(2):
         for part in range(2):
             real = tab[which, 2 * part]
@@ -212,10 +234,29 @@
 
     @pl.when(pair == 0)
     def _():
-        psi[0] = ill[...]
-
-    def own_rows(row):
-        cells = lax.broadcasted_iota(jnp.int32, (width, half), 0)
+        i0 = lax.broadcasted_iota(jnp.int32, (width, width), 0)
+        i1 = lax.broadcasted_iota(jnp.int32, (width, width), 1)
+        row = pos[0, 0:1, 0:1]
+        col = pos[1, 0:1, 0:1]
+        place_r = jnp.where(((i1 + row + half) & (width - 1)) == i0, 1.0, 0.0)
+        place_c = jnp.where(((i0 + col + half) & (width - 1)) == i1, 1.0, 0.0)
+        place_r = place_r.astype(jnp.bfloat16)
+        place_c = place_c.astype(jnp.bfloat16)
+
+        def thirds(value):
+            high, middle = split(value)
+            rest = value - high.astype(jnp.float32) - middle.astype(jnp.float32)
+            return high, middle, rest.astype(jnp.bfloat16)
+
+        for part in range(2):
+            high, middle, low = thirds(ill[part])
+            value = dot(place_r, high) + dot(place_r, middle) + dot(place_r, low)
+            high, middle, low = thirds(value)
+            psi[0, part] = dot(high, place_c) + dot(middle, place_c) + dot(low, place_c)
+
+    def own_rows(row, h):
+        shape = (width if h is None else half, half)
+        cells = lax.broadcasted_iota(jnp.int32, shape, 0) + (h or 0) * half
         return (cells >= row - half) & (cells < row + half)
 
     def own_cols(side):
@@ -223,29 +264,31 @@
         col = pos[1, 0:1, 0:half]
         return (cells >= col - half) & (cells < col + half)
 
-    def my_rows():
-        return own_rows(pos[0, 0:1, 0:half])
-
-    def their_rows(slot):
-        return own_rows(posbuf[slot, 0, 0:1, 0:half])
+    def my_rows(h=None):
+        return own_rows(pos[0, 0:1, 0:half], h)
+
+    def their_rows(slot, h):
+        return own_rows(posbuf[slot, 0, 0:1, 0:half], h)
 
     sides = (slice(0, half), slice(half, width))
 
     for copy in pos_copies():
         copy.wait_recv()
 
+    obj_copy.wait()
+
     def send_columns(s, carry):
         for part in range(2):
-            for copy in y_copies(s, part):
-                copy.wait_recv()
-            for side in range(2):
-                zs[s, side, part] = jnp.where(
-                    their_rows(side),
-                    obj[s, part, :, sides[side]],
-                    ybuf[s, part, :, sides[side]],
-                )
-            for copy in z_copies(s, part):
-                copy.start()
+            for h in range(2):
+                y_copies(s, part)[h].wait_recv()
+                for side in range(2):
+                    zs[s, side, part, sides[h]] = jnp.where(
+                        their_rows(side, h),
+                        obj[s, part, sides[h], sides[side]],
+                        ybuf[s, part, sides[h], sides[side]],
+                    )
+                for copy in z_copies(s, part, h):
+                    copy.start()
         return carry
 
     lax.fori_loop(0, layers, send_columns, 0)
@@ -281,7 +324,7 @@
 
     def build_window(s, carry):
         for c in range(2):
-            for copy in z_copies(s, c):
+            for copy in z_copies(s, c, 0) + z_copies(s, c, 1):
                 copy.wait_recv()
         rows = my_rows()
         at = core * layers + s
@@ -345,7 +388,7 @@
                     here = terms[part][:, sides[side]]
                     gzs[s, side, part] = jnp.where(cols, 0.0, here)
                     term[s, part, :, sides[side]] = jnp.where(cols, here, 0.0)
-                for copy in gz_copies(s, part):
+                for copy in gz_copies(s, part, 0) + gz_copies(s, part, 1):
                     copy.start()
 
         return carry
@@ -355,21 +398,21 @@
     def send_rows(step, carry):
         s = layers - 1 - step
         for part in range(2):
-            for copy in gz_copies(s, part):
-                copy.wait_recv()
-            rows = my_rows()
-            for side in range(2):
-                theirs = their_rows(side)
-                mine = term[s, part, :, sides[side]]
-                came = gzr[s, side, part]
-                gys[s, part, :, sides[side]] = jnp.where(rows, 0.0, mine) + jnp.where(
-                    theirs, 0.0, came
-                )
-                term[s, part, :, sides[side]] = jnp.where(rows, mine, 0.0) + jnp.where(
-                    theirs, came, 0.0
-                )
-            for copy in gy_copies(s, part):
-                copy.start()
+            for h in range(2):
+                for copy in gz_copies(s, part, h):
+                    copy.wait_recv()
+                rows = my_rows(h)
+                for side in range(2):
+                    theirs = their_rows(side, h)
+                    mine = term[s, part, sides[h], sides[side]]
+                    came = gzr[s, side, part, sides[h]]
+                    gys[s, part, sides[h], sides[side]] = jnp.where(
+                        rows, 0.0, mine
+                    ) + jnp.where(theirs, 0.0, came)
+                    term[s, part, sides[h], sides[side]] = jnp.where(
+                        rows, mine, 0.0
+                    ) + jnp.where(theirs, came, 0.0)
+                gy_copies(s, part)[h].start()
         return carry
 
     lax.fori_loop(0, layers, send_rows, 0)
@@ -387,9 +430,12 @@
     for copy in pos_copies():
         copy.wait_send()
     for s in range(layers):
-        for copies in (y_copies, z_copies, gz_copies, gy_copies):
-            for copy in copies(s, 0) + copies(s, 1):
+        for c in range(2):
+            for copy in y_copies(s, c) + gy_copies(s, c):
                 copy.wait_send()
+            for h in range(2):
+                for copy in z_copies(s, c, h) + gz_copies(s, c, h):
+                    copy.wait_send()
 
         window_copy(s).wait_send()
 
@@ -412,22 +458,26 @@
     half = width // 2
     counts = tuple(lax.axis_size(a) for a in ("tx", "ty", "sl"))
     offset = positions.reshape(2)
-    rolled = jnp.roll(illumination, (offset[0] - half, offset[1] - half), axis=(1, 2))
     pos = jnp.broadcast_to(offset[:, None, None], (2, 8, half)).astype(jnp.int32)
     tables = jnp.asarray(build_tables(width))
     f32 = jnp.float32
     wave = (layers, 2, width, width)
     strips = (layers, 2, 2, width, half)
     pairs = pltpu.SemaphoreType.DMA((layers, 2, 2))
+    quads = pltpu.SemaphoreType.DMA((layers, 2, 2, 2))
     two = pltpu.SemaphoreType.DMA((2,))
     square = pltpu.SemaphoreType.DMA((2, 2))
     windows = pltpu.SemaphoreType.DMA((layers,))
     return pl.pallas_call(
         functools.partial(kernel, counts),
         out_shape=jax.ShapeDtypeStruct(object_field.shape, f32),
-        in_specs=[pl.BlockSpec(memory_space=pltpu.VMEM)] * 5,
+        in_specs=[pl.BlockSpec(memory_space=pl.ANY)]
+        + [pl.BlockSpec(memory_space=pltpu.VMEM)] * 3
+        + [pl.BlockSpec(memory_space=pl.ANY)],
         out_specs=pl.BlockSpec(memory_space=pltpu.VMEM),
         scratch_shapes=[
+            pltpu.VMEM(wave, f32),
+            pltpu.VMEM(tables.shape, jnp.bfloat16),
             pltpu.VMEM((2, 4 * width, 2 * width), jnp.bfloat16),
             pltpu.VMEM((2, 2, 2 * width, 2 * width), jnp.bfloat16),
             pltpu.VMEM(wave, f32),
@@ -443,14 +493,17 @@
             pltpu.VMEM(wave, f32),
             pltpu.VMEM((2, 2, 8, half), jnp.int32),
         ]
-        + [pairs] * 8
+        + [pairs] * 2
+        + [quads] * 4
+        + [pairs] * 2
         + [two] * 2
         + [square] * 4
-        + [windows] * 2,
+        + [windows] * 2
+        + [two],
         compiler_params=pltpu.CompilerParams(
             collective_id=0, has_side_effects=True, vmem_limit_bytes=48 * 1024 * 1024
         ),
-    )(object_field, rolled, pos, measured.reshape(width, width), tables)
+    )(object_field, illumination, pos, measured.reshape(width, width), tables)
 
 
 def solution(mesh):

time: 114 us -> 110 us (0.965)
  Pallas kernels: 107 us -> 104 us
  local copies, waits for them, and re-layouts: 3.24 us -> 6.14 us
  other arithmetic: 1.71 us -> 0 us
  between operations: 1.36 us -> 0.01 us
    pallas_call x1, Pallas kernels: 107 us -> 104 us  [body(): pl.pallas_call(functools.partial(kernel, counts), out_shape=jax.ShapeDtyp...]
    unnamed x9 -> x11, local copies, waits for them, and re-layouts: 2.58 us -> 6.07 us
    concatenate x2 -> x0, other arithmetic: 1.71 us -> none  [body(): jnp.roll(illumination, (offset[0] - half, offset[1] - half), axis=(1, 2))]
where the time goes in v4:
time: 110 us
  Pallas kernels  104 us (95%)
  local copies, waits for them, and re-layouts  6.14 us (6%)
    pallas_call x1, Pallas kernels, body(): pl.pallas_call(functools.partial(kernel, counts), out_shape=jax.ShapeDtyp...  104 us
    unnamed x11, local copies, waits for them, and re-layouts  6.07 us

profile of v4, /device:TPU:0, one launch (start us, length us, event | category | flops | bytes accessed | tf_op | source)
XLA Modules:
  0.0 109.7 jit_solution(6355933065331741578)
XLA Ops:
  0.0 0.0 copy-start.4
  0.0 0.7 copy-done.4
  0.7 0.1 broadcast_in_dim.8.pos
  0.7 0.0 copy-start
  0.7 1.2 %copy-done = f32[2,2,256,256]{3,2,1,0:T(8,128)S(1)} copy-done((f32[2,2,256,256]{3,2,1,0:T(8,128)S(1)}, f32[2,2,256,256]{3,2,1,0:T(8,128)}, u32[]{:S(2)}) %copy-start) | copy-done | bytes 1048600
  2.0 0.0 copy-start.1
  2.0 1.2 %copy-done.1 = bf16[2,4,256,256]{3,2,1,0:T(8,128)(2,1)S(1)} copy-done((bf16[2,4,256,256]{3,2,1,0:T(8,128)(2,1)S(1)}, bf16[2,4,256,256]{3,2,1,0:T(8,128)(2,1)}, u32[]{:S(2)}) %copy-start.1) | copy-done | bytes 1048600
  3.2 0.0 copy-start.2
  3.2 1.0 copy-done.2
  4.2 0.0 copy-start.3
  4.2 0.9 copy-done.3
  5.2 103.5 %shard_map.55 = f32[2,2,256,256]{3,2,1,0:T(8,128)S(1)} custom-call(f32[2,2,256,256]{3,2,1,0:T(8,128)S(1)} %copy-done, f32[2,256,256]{2,1,0:T(8,128)S(1)} %copy-done.2, s32[2,8,128]{2,1,0:T(8,128)S(1)} %broadcast_in_dim.8.pos, f32[256,256]{1,0:T(8,128)S(1)} %bitcast.2, bf16[2,4,256,256]{3,2,1,0:T(8,128)(2,1)S(1)} %copy-done.1), custom_call_target="tpu_custom_call" | custom-call | tf_op jit(solution)/shard_map/pallas_call | solution.py:471
  108.7 1.0 copy.7
Async XLA Ops:
  0.0 0.7 copy-start.4
  0.7 1.2 %copy-start = (f32[2,2,256,256]{3,2,1,0:T(8,128)S(1)}, f32[2,2,256,256]{3,2,1,0:T(8,128)}, u32[]{:S(2)}) copy-start(f32[2,2,256,256]{3,2,1,0:T(8,128)} %obj_in.1) | copy-start | bytes 3145732
  2.0 1.2 %copy-start.1 = (bf16[2,4,256,256]{3,2,1,0:T(8,128)(2,1)S(1)}, bf16[2,4,256,256]{3,2,1,0:T(8,128)(2,1)}, u32[]{:S(2)}) copy-start(bf16[2,4,256,256]{3,2,1,0:T(8,128)(2,1)} %constant.2.clone.tab_in) | copy-start | bytes 3145732
  3.2 1.0 copy-start.2
  4.2 0.9 copy-start.3
